TPU v7x, 32 devices: a whole 2x2x4 slice. The times are simulated.
32 devices in a mesh: group: 2 (over x), sample: 16 (over z, y, core).
Axes of the slice: x: 2, y: 2, z: 4, core: 2. Of those that a mesh axis runs over, the one named last changes fastest.
Arguments:
- queries: bfloat16 [32, 3, 64, 128], P(('group', 'sample')), parts along dimension 0, may hold values from -150 to 150
- prefix_keys: bfloat16 [4096, 8, 128], P(('group', 'sample')), parts along dimension 0, may hold values from -5 to 5
- prefix_values: bfloat16 [4096, 8, 128], P(('group', 'sample')), parts along dimension 0, may hold values from -6 to 6
- suffix_keys: bfloat16 [32, 1024, 8, 128], P(('group', 'sample')), parts along dimension 0, may hold values from -7 to 7
- suffix_values: bfloat16 [32, 1024, 8, 128], P(('group', 'sample')), parts along dimension 0, may hold values from -6 to 6
- suffix_lengths: int32 [32], P(('group', 'sample')), parts along dimension 0, may hold values from 0 to 1024, as said below
- new_keys: bfloat16 [32, 3, 8, 128], P(('group', 'sample')), parts along dimension 0, may hold values from -5 to 5
- new_values: bfloat16 [32, 3, 8, 128], P(('group', 'sample')), parts along dimension 0, may hold values from -6 to 6
Outputs:
- attention: float32 [32, 3, 64, 128], P(('group', 'sample')), parts along dimension 0
There are 2 independent parts, one for each index of `group`. A program takes and returns all parts, laid end to end along the dimension named above; each array names one. Nothing has to cross between parts.
Inputs may be any that keep to these rules, and one draw needn't show every extreme that they name: `suffix_lengths`: some sample of every group has exactly 1024 generated tokens.
All inputs are finite; a program needn't handle non-finite values.
Results may differ from a plain program's by a relative error of at most 0.00042.
Values may be sent and summed in bfloat16 or wider, within the bound.
A program may use at most 128 MiB of HBM per device.

v0:
```python
import functools
import math

import jax
import jax.numpy as jnp
from jax import lax
from jax.experimental import pallas as pl
from jax.experimental.pallas import tpu as pltpu
from jax.sharding import PartitionSpec as P

F32, BF16 = jnp.float32, jnp.bfloat16


def rows_of(tiles):
    wide = tiles.astype(F32)
    return wide.reshape(math.prod(wide.shape[:-1]), wide.shape[-1])


def nt_dot(a, b):
    return lax.dot_general(a, b, (((1,), (1,)), ((), ())), preferred_element_type=F32)


def kernel(
    n, group, chunk,
    len_hbm, q_hbm, pk_hbm, pv_hbm, sk_hbm, sv_hbm, nk_hbm, nv_hbm,
    out_ref,
    q_own, pk, pv, wide, k_send, v_send, q_all, k_all, v_all, sk, sv, nk, nv, s_own,
    o_send, l_send, o_all, l_all, len_own, w_high, w_low, total_all,
    local_sem, suf_sem, q_ss, q_rs, k_ss, k_rs, v_ss, v_rs, o_ss, o_rs, l_ss, l_rs,
):
    steps, kvh, gsize, dim = q_hbm.shape
    per = steps * gsize
    tokens = pk.shape[0] // kvh
    factor = 1.0 / math.sqrt(dim)
    me = lax.axis_index("sample")
    head = lax.rem(me, kvh)
    base = me - head
    chunks = sk.shape[0] // chunk

    def remote(src, dst, ss, rs, dev):
        return pltpu.make_async_remote_copy(
            src_ref=src, dst_ref=dst, send_sem=ss, recv_sem=rs,
            device_id={"sample": dev}, device_id_type=pl.DeviceIdType.MESH,
        )

    local = [
        pltpu.make_async_copy(a, b, local_sem.at[i])
        for i, (a, b) in enumerate(
            [(pk_hbm, pk), (pv_hbm, pv), (q_hbm, q_own), (nk_hbm, nk), (nv_hbm, nv), (len_hbm, len_own)]
        )
    ]
    for c in local:
        c.start()
    own_q = pltpu.make_async_copy(q_hbm.at[:, head], q_all.at[me], q_rs.at[me])
    own_q.start()
    halves = []
    for i, (a, b) in enumerate([(sk_hbm, sk), (sv_hbm, sv)]):
        for c in range(chunks):
            part = pl.ds(c * chunk, chunk)
            halves.append(
                pltpu.make_async_copy(a.at[part], b.at[part], suf_sem.at[i * chunks + c])
            )
    for c in halves:
        c.start()

    barrier = pltpu.get_barrier_semaphore()

    def greet(d, _):
        pl.semaphore_signal(
            barrier, inc=1, device_id={"sample": lax.rem(me + d, n)},
            device_id_type=pl.DeviceIdType.MESH,
        )
        return 0

    lax.fori_loop(1, n, greet, 0)

    for src, copy, dst, mine in ((pk, local[0], k_send, k_all), (pv, local[1], v_send, v_all)):
        copy.wait()
        wide[...] = src[...].astype(F32)
        for h in range(kvh):
            dst[h] = wide[pl.ds(h, tokens, stride=kvh), :].astype(BF16)
        mine[head] = wide[pl.ds(head, tokens, stride=kvh), :].astype(BF16)

    pl.semaphore_wait(barrier, n - 1)

    def q_copy(d):
        dev = lax.rem(me + d, n)
        return remote(q_hbm.at[:, lax.rem(dev, kvh)], q_all.at[me], q_ss.at[d], q_rs.at[me], dev)

    def kv_copy(d, src, dst, ss, rs):
        hd = lax.rem(head + d, kvh)
        return remote(src.at[hd], dst.at[head], ss.at[d], rs.at[head], base + hd)

    def start(copy):
        def body(d, _):
            copy(d).start()
            return 0
        return body

    k_copy = lambda d: kv_copy(d, k_send, k_all, k_ss, k_rs)
    v_copy = lambda d: kv_copy(d, v_send, v_all, v_ss, v_rs)
    lax.fori_loop(1, n, start(q_copy), 0)
    lax.fori_loop(1, kvh, start(k_copy), 0)
    lax.fori_loop(1, kvh, start(v_copy), 0)

    for c in local[2:]:
        c.wait()
    rows = kvh * per
    q_rows = jnp.concatenate(
        [q_own[t, h].astype(F32) for h in range(kvh) for t in range(steps)], axis=0
    ).astype(BF16)
    length = len_own[0]
    row = lax.broadcasted_iota(jnp.int32, (rows, 128), 0)
    lane = lax.broadcasted_iota(jnp.int32, (rows, 128), 1)
    lane_head = lax.rem(lane, kvh)
    match = (row >= lane_head * per) & (row < (lane_head + 1) * per)
    bias = jnp.where(match, 0.0, -jnp.inf).astype(F32)
    bias_wide = jnp.concatenate([bias] * (chunk // 128), axis=1)
    token_of = lax.div(lax.broadcasted_iota(jnp.int32, (8, chunk), 1), kvh)

    top = jnp.full((rows, 1), -jnp.inf, F32)
    for c in range(chunks):
        halves[c].wait()
        s = nt_dot(q_rows, sk[c * chunk:(c + 1) * chunk, :]) * factor
        limit = jnp.where(token_of < length - c * (chunk // kvh), 0.0, -jnp.inf).astype(F32)[:1]
        s = s + bias_wide + limit
        s_own[c] = s
        top = jnp.maximum(top, jnp.max(s, axis=-1, keepdims=True))

    pad = jnp.zeros((128 - steps * kvh, dim), F32)
    new_k = jnp.concatenate([nk[j].astype(F32) for j in range(steps)] + [pad], axis=0).astype(BF16)
    new_v = jnp.concatenate([nv[j].astype(F32) for j in range(steps)] + [pad], axis=0).astype(BF16)
    step_of = lax.div(lax.rem(row, per), gsize)
    s_new = nt_dot(q_rows, new_k) * factor + bias
    s_new = jnp.where(lax.div(lane, kvh) <= step_of, s_new, -jnp.inf)
    own_max = jnp.maximum(top, jnp.max(s_new, axis=-1, keepdims=True))
    w_new = jnp.exp(s_new - own_max)
    own_total = jnp.sum(w_new, axis=-1, keepdims=True)
    own_sum = jnp.dot(w_new.astype(BF16), new_v, preferred_element_type=F32)
    for c in range(chunks):
        halves[chunks + c].wait()
        w = jnp.exp(s_own[c] - own_max)
        own_total = own_total + jnp.sum(w, axis=-1, keepdims=True)
        own_sum = own_sum + jnp.dot(
            w.astype(BF16), sv[c * chunk:(c + 1) * chunk, :], preferred_element_type=F32
        )

    own_q.wait()

    def arrive(make, rs):
        def body(d, _):
            make(d, rs).wait_recv()
            return 0
        return body

    def q_in(d, _):
        src = lax.rem(me + d, n)
        return remote(q_hbm.at[:, head], q_all.at[src], q_ss.at[d], q_rs.at[src], src)

    def kv_in(src, dst, ss, rs):
        def make(d, _):
            hd = lax.rem(head + d, kvh)
            return remote(src.at[hd], dst.at[hd], ss.at[d], rs.at[hd], base + hd)
        return make

    lax.fori_loop(1, n, arrive(q_in, None), 0)
    lax.fori_loop(1, kvh, arrive(kv_in(k_send, k_all, k_ss, k_rs), None), 0)

    diag_row = lax.broadcasted_iota(jnp.int32, (per, 128), 0)
    diag_lane = lax.broadcasted_iota(jnp.int32, (per, 128), 1)
    diag = diag_row == diag_lane

    def out_copy(dev):
        return remote(o_send.at[dev], o_all.at[me], o_ss.at[dev], o_rs.at[me], dev)

    def log_copy(dev):
        return remote(l_send.at[dev], l_all.at[me], l_ss.at[dev], l_rs.at[me], dev)

    keys = k_all[...].reshape(kvh * tokens, dim)
    groups = n // group
    span = group * per

    def first_of(i):
        return lax.rem(base + kvh + i * group, n)

    def weigh(i, _):
        first = first_of(i)
        at = pl.ds(pl.multiple_of(first * per, span), span)
        q_block = rows_of(q_all[pl.ds(first, group)]).astype(BF16)
        s = nt_dot(q_block, keys) * factor
        m = jnp.max(s, axis=-1, keepdims=True)
        w = jnp.exp(s - m)
        total = jnp.sum(w, axis=-1, keepdims=True)
        high = w.astype(BF16)
        w_high[at] = high
        w_low[at] = (w - high.astype(F32)).astype(BF16)
        total_all[at] = total
        logs = jnp.broadcast_to(m + jnp.log(total), (span, 128)).reshape(group, per, 128)
        l_send[pl.ds(first, group)] = jnp.sum(
            jnp.where(diag[None], logs, 0.0), axis=1, keepdims=True
        )
        for j in range(group):
            dev = first + j

            @pl.when(dev != me)
            def _():
                log_copy(dev).start()

        return 0

    lax.fori_loop(0, groups, weigh, 0)
    lax.fori_loop(1, kvh, arrive(kv_in(v_send, v_all, v_ss, v_rs), None), 0)
    values = v_all[...].reshape(kvh * tokens, dim)

    def block(i, _):
        first = first_of(i)
        at = pl.ds(pl.multiple_of(first * per, span), span)
        sums = jnp.dot(w_high[at], values, preferred_element_type=F32) + jnp.dot(
            w_low[at], values, preferred_element_type=F32
        )
        o_send[pl.ds(first, group)] = (sums / total_all[at]).reshape(group, per, dim)
        for j in range(group):
            dev = first + j

            @pl.when(dev != me)
            def _():
                out_copy(dev).start()

        return 0

    lax.fori_loop(0, groups, block, 0)
    mine_o = pltpu.make_async_copy(o_send.at[me], o_all.at[me], o_rs.at[me])
    mine_l = pltpu.make_async_copy(l_send.at[me], l_all.at[me], l_rs.at[me])
    mine_o.start()
    mine_l.start()

    def drain(d, _):
        q_copy(d).wait_send()
        return 0

    def drain_kv(d, _):
        k_copy(d).wait_send()
        v_copy(d).wait_send()
        return 0

    lax.fori_loop(1, n, drain, 0)
    lax.fori_loop(1, kvh, drain_kv, 0)
    mine_o.wait()
    mine_l.wait()

    def results_in(d, _):
        src = lax.rem(me + d, n)
        remote(o_send.at[src], o_all.at[src], o_ss.at[src], o_rs.at[src], src).wait_recv()
        remote(l_send.at[src], l_all.at[src], l_ss.at[src], l_rs.at[src], src).wait_recv()
        return 0

    lax.fori_loop(1, n, results_in, 0)

    repeats = n // kvh
    logs = jnp.sum(
        jnp.where(diag[None], jnp.broadcast_to(l_all[...], (n, per, 128)), 0.0),
        axis=-1, keepdims=True,
    ).reshape(repeats, rows, 1)
    largest = jnp.maximum(jnp.max(logs, axis=0), own_max)
    weights = jnp.exp(logs - largest[None])
    share = jnp.exp(own_max - largest)
    upper = share * own_sum
    lower = share * own_total
    for r in range(repeats):
        piece = o_all[r * kvh:(r + 1) * kvh].reshape(rows, dim)
        upper = upper + weights[r] * piece
        lower = lower + weights[r]
    result = upper / lower
    for h in range(kvh):
        for t in range(steps):
            at = h * per + t * gsize
            out_ref[t, h] = result[at:at + gsize]

    def drain_out(d, _):
        dev = lax.rem(me + d, n)
        out_copy(dev).wait_send()
        log_copy(dev).wait_send()
        return 0

    lax.fori_loop(1, n, drain_out, 0)


def solution(mesh):
    n = mesh.shape["sample"]

    def shards(queries, pk, pv, sk, sv, lengths, nk, nv):
        _, steps, heads, dim = queries.shape
        tokens, kvh, _ = pk.shape
        gsize = heads // kvh
        suffix = sk.shape[1]
        per = steps * gsize
        group = math.gcd(n, 4)
        chunk = math.gcd(suffix * kvh, 1024)
        chunks = suffix * kvh // chunk
        any_spec = pl.BlockSpec(memory_space=pl.ANY)
        dma = pltpu.SemaphoreType.DMA
        out = pl.pallas_call(
            functools.partial(kernel, n, group, chunk),
            out_shape=jax.ShapeDtypeStruct((steps, kvh, gsize, dim), F32),
            in_specs=[any_spec] + [pl.BlockSpec(memory_space=pltpu.HBM)] * 7,
            out_specs=pl.BlockSpec(memory_space=pltpu.VMEM),
            scratch_shapes=[
                pltpu.VMEM((steps, kvh, gsize, dim), BF16),
                pltpu.VMEM((tokens * kvh, dim), BF16),
                pltpu.VMEM((tokens * kvh, dim), BF16),
                pltpu.VMEM((tokens * kvh, dim), F32),
                pltpu.VMEM((kvh, tokens, dim), BF16),
                pltpu.VMEM((kvh, tokens, dim), BF16),
                pltpu.VMEM((n, steps, gsize, dim), BF16),
                pltpu.VMEM((kvh, tokens, dim), BF16),
                pltpu.VMEM((kvh, tokens, dim), BF16),
                pltpu.VMEM((suffix * kvh, dim), BF16),
                pltpu.VMEM((suffix * kvh, dim), BF16),
                pltpu.VMEM((steps, kvh, dim), BF16),
                pltpu.VMEM((steps, kvh, dim), BF16),
                pltpu.VMEM((chunks, kvh * per, chunk), F32),
                pltpu.VMEM((n, per, dim), F32),
                pltpu.VMEM((n, 1, 128), F32),
                pltpu.VMEM((n, per, dim), F32),
                pltpu.VMEM((n, 1, 128), F32),
                pltpu.SMEM((1,), jnp.int32),
                pltpu.VMEM((n * per, kvh * tokens), BF16),
                pltpu.VMEM((n * per, kvh * tokens), BF16),
                pltpu.VMEM((n * per, 1), F32),
                dma((6,)), dma((2 * chunks,)),
                dma((n,)), dma((n,)), dma((kvh,)), dma((kvh,)), dma((kvh,)), dma((kvh,)),
                dma((n,)), dma((n,)), dma((n,)), dma((n,)),
            ],
            compiler_params=pltpu.CompilerParams(
                collective_id=0, has_side_effects=True, vmem_limit_bytes=48 << 20
            ),
        )(lengths, *[pltpu.with_memory_space_constraint(x, pltpu.HBM) for x in (
            queries.reshape(steps, kvh, gsize, dim),
            pk.reshape(tokens * kvh, dim),
            pv.reshape(tokens * kvh, dim),
            sk.reshape(suffix * kvh, dim),
            sv.reshape(suffix * kvh, dim),
            nk.reshape(steps, kvh, dim),
            nv.reshape(steps, kvh, dim),
        )])
        return out.reshape(1, steps, heads, dim)

    spread = ("group", "sample")
    four = P(spread, None, None, None)
    three = P(spread, None, None)
    return jax.shard_map(
        shards, mesh=mesh,
        in_specs=(four, three, three, four, four, P(spread), four, four),
        out_specs=four, check_vma=False,
    )
```

profile of v0, /device:TPU:0, one launch (start us, length us, event | category | flops | bytes accessed | tf_op | source)
XLA Modules:
  0.0 23.1 jit_solution(9605559242247829420)
XLA Ops:
  0.7 21.8 %shard_map.82 = f32[3,8,8,128]{3,2,1,0:T(8,128)S(1)} custom-call(s32[1]{0:T(128)S(6)} %copy.10.len_hbm, bf16[3,8,8,128]{3,2,1,0:T(8,128)(2,1)} %bitcast.13, bf16[1024,128]{1,0:T(8,128)(2,1)} %bitcast.11, bf16[1024,128]{1,0:T(8,128)(2,1)} %bitcast.12, bf16[8192,128]{1,0:T(8,128)(2,1)} %bitcast.9, bf16[8192,128]{1,0:T(8,128)(2,1)} %bitcast.10, ...), custom_call_target="tpu_custom_call" | custom-call | tf_op jit(solution)/shard_map/pallas_call | solution.py:302
  22.4 0.6 %copy.11 = f32[1,3,64,128]{3,2,1,0:T(8,128)} copy(f32[1,3,64,128]{3,2,1,0:T(8,128)S(1)} %bitcast.8) | data formatting | bytes 196608
where the time goes:
time: 23.2 us; the launch traced here: 23.1 us
  Pallas kernels  21.8 us (94%)
  between operations  0.66 us (3%)
  local copies, waits for them, and re-layouts  0.64 us (3%)
    pallas_call x1, Pallas kernels, shards(): pl.pallas_call(functools.partial(kernel, n, group, chunk), out_shape=jax....  21.8 us
    unnamed x1, local copies, waits for them, and re-layouts  0.64 us

commit v1 on v0

v1 whole, which is shorter than its diff:
```python
import functools
import math

import jax
import jax.numpy as jnp
from jax import lax
from jax.experimental import pallas as pl
from jax.experimental.pallas import tpu as pltpu
from jax.sharding import PartitionSpec as P

F32, BF16, I16 = jnp.float32, jnp.bfloat16, jnp.int16
STEPS_OF_CODE = 32767.0


def rows_of(tiles):
    wide = tiles.astype(F32)
    return wide.reshape(math.prod(wide.shape[:-1]), wide.shape[-1])


def nt_dot(a, b):
    return lax.dot_general(a, b, (((1,), (1,)), ((), ())), preferred_element_type=F32)


def kernel(
    n, group, chunk,
    lens, q_hbm, pk_hbm, pv_hbm, sk_hbm, sv_hbm, nk_hbm, nv_hbm,
    out_ref,
    q_own, pk, pv, wide, k_send, v_send, q_all, k_all, v_all, sk, sv, nk, nv, s_own,
    o_send, l_send, o_all, l_all, w_high, w_low, log_all, total_all,
    local_sem, suf_sem, block_sem, q_ss, q_rs, k_ss, k_rs, v_ss, v_rs, o_ss, o_rs, l_ss, l_rs,
):
    steps, kvh, gsize, dim = q_hbm.shape
    per = steps * gsize
    tokens = pk.shape[0] // kvh
    factor = 1.0 / math.sqrt(dim)
    me = lax.axis_index("sample")
    head = lax.rem(me, kvh)
    mine = lax.div(me, kvh)
    base = me - head
    chunks = sk.shape[0] // chunk
    blocks = n // kvh

    def remote(src, dst, ss, rs, dev):
        return pltpu.make_async_remote_copy(
            src_ref=src, dst_ref=dst, send_sem=ss, recv_sem=rs,
            device_id={"sample": dev}, device_id_type=pl.DeviceIdType.MESH,
        )

    def signal(sem, dev):
        pl.semaphore_signal(
            sem, inc=1, device_id={"sample": dev}, device_id_type=pl.DeviceIdType.MESH
        )

    def repeat(first, last, action):
        def body(d, _):
            action(d)
            return 0
        lax.fori_loop(first, last, body, 0)

    barrier = pltpu.get_barrier_semaphore()
    paired = blocks == 2
    second = base > 0
    other = lax.rem(base + kvh, n)
    if paired:
        repeat(1, kvh, lambda d: signal(barrier, base + lax.rem(head + d, kvh)))

        @pl.when(jnp.logical_not(second))
        def _():
            repeat(0, kvh, lambda d: signal(barrier, other + lax.rem(head + d, kvh)))
    else:
        repeat(1, n, lambda d: signal(barrier, lax.rem(me + d, n)))

    local = [
        pltpu.make_async_copy(a, b, local_sem.at[i])
        for i, (a, b) in enumerate(
            [(pk_hbm, pk), (pv_hbm, pv), (q_hbm, q_own), (nk_hbm, nk), (nv_hbm, nv)]
        )
    ]
    for c in local:
        c.start()
    own_q = pltpu.make_async_copy(q_hbm.at[:, head], q_all.at[me], q_rs.at[mine])
    own_q.start()
    halves = []
    for i, (a, b) in enumerate([(sk_hbm, sk), (sv_hbm, sv)]):
        for c in range(chunks):
            part = pl.ds(c * chunk, chunk)
            halves.append(
                pltpu.make_async_copy(a.at[part], b.at[part], suf_sem.at[i * chunks + c])
            )
    for c in halves:
        c.start()

    def split(src, copy, dst, kept):
        copy.wait()
        wide[...] = src[...].astype(F32)
        for h in range(kvh):
            dst[h] = wide[pl.ds(h, tokens, stride=kvh), :].astype(BF16)
        kept[head] = wide[pl.ds(head, tokens, stride=kvh), :].astype(BF16)

    def send_q(dev):
        remote(q_hbm.at[:, lax.rem(dev, kvh)], q_all.at[me], q_ss, q_rs.at[mine], dev).start()

    def send_kv(d, src, dst, ss, rs):
        hd = lax.rem(head + d, kvh)
        remote(src.at[hd], dst.at[head], ss, rs, base + hd).start()

    def near_q(d):
        send_q(base + lax.rem(head + d, kvh))

    def far_q(d):
        send_q(lax.rem(base + kvh + lax.rem(head + d, kvh) + lax.div(d, kvh) * kvh, n))

    def all_far_q():
        repeat(0, n - kvh, far_q)

    if paired:
        @pl.when(second)
        def _():
            pl.semaphore_wait(barrier, n - 1)
            repeat(0, kvh, lambda d: signal(block_sem, other + lax.rem(head + d, kvh)))
            all_far_q()

        @pl.when(jnp.logical_not(second))
        def _():
            pl.semaphore_wait(barrier, kvh - 1)
    else:
        pl.semaphore_wait(barrier, n - 1)
        all_far_q()
    repeat(1, kvh, near_q)
    split(pk, local[0], k_send, k_all)
    repeat(1, kvh, lambda d: send_kv(d, k_send, k_all, k_ss, k_rs))
    split(pv, local[1], v_send, v_all)
    if paired:
        @pl.when(jnp.logical_not(second))
        def _():
            pl.semaphore_wait(block_sem, kvh)
            all_far_q()
    repeat(1, kvh, lambda d: send_kv(d, v_send, v_all, v_ss, v_rs))

    for c in local[2:]:
        c.wait()
    rows = kvh * per
    q_rows = jnp.concatenate(
        [q_own[t, h].astype(F32) for h in range(kvh) for t in range(steps)], axis=0
    ).astype(BF16)
    length = lens[0]
    row = lax.broadcasted_iota(jnp.int32, (rows, 128), 0)
    lane = lax.broadcasted_iota(jnp.int32, (rows, 128), 1)
    lane_head = lax.rem(lane, kvh)
    match = (row >= lane_head * per) & (row < (lane_head + 1) * per)
    bias = jnp.where(match, 0.0, -jnp.inf).astype(F32)
    bias_wide = jnp.concatenate([bias] * (chunk // 128), axis=1)
    token_of = lax.div(lax.broadcasted_iota(jnp.int32, (8, chunk), 1), kvh)

    top = jnp.full((rows, 1), -jnp.inf, F32)
    for c in range(chunks):
        halves[c].wait()
        s = nt_dot(q_rows, sk[c * chunk:(c + 1) * chunk, :]) * factor
        limit = jnp.where(token_of < length - c * (chunk // kvh), 0.0, -jnp.inf).astype(F32)[:1]
        s = s + bias_wide + limit
        s_own[c] = s
        top = jnp.maximum(top, jnp.max(s, axis=-1, keepdims=True))

    pad = jnp.zeros((128 - steps * kvh, dim), F32)
    new_k = jnp.concatenate([nk[j].astype(F32) for j in range(steps)] + [pad], axis=0).astype(BF16)
    new_v = jnp.concatenate([nv[j].astype(F32) for j in range(steps)] + [pad], axis=0).astype(BF16)
    step_of = lax.div(lax.rem(row, per), gsize)
    s_new = nt_dot(q_rows, new_k) * factor + bias
    s_new = jnp.where(lax.div(lane, kvh) <= step_of, s_new, -jnp.inf)
    own_max = jnp.maximum(top, jnp.max(s_new, axis=-1, keepdims=True))
    w_new = jnp.exp(s_new - own_max)
    own_total = jnp.sum(w_new, axis=-1, keepdims=True)
    own_sum = jnp.dot(w_new.astype(BF16), new_v, preferred_element_type=F32)
    for c in range(chunks):
        halves[chunks + c].wait()
        w = jnp.exp(s_own[c] - own_max)
        own_total = own_total + jnp.sum(w, axis=-1, keepdims=True)
        own_sum = own_sum + jnp.dot(
            w.astype(BF16), sv[c * chunk:(c + 1) * chunk, :], preferred_element_type=F32
        )

    def settle(ref, sem):
        pltpu.make_async_copy(ref, ref, sem).wait()

    def others(ref):
        return ref.at[pl.ds(0, kvh - 1)]

    settle(others(k_all), k_rs)
    keys = k_all[...].reshape(kvh * tokens, dim)
    groups = kvh // group
    span = group * per

    def place(block, i):
        first = block * kvh + i * group
        return first, pl.ds(pl.multiple_of(first * per, span), span)

    def weigh(block):
        settle(q_all.at[pl.ds(block * kvh, kvh)], q_rs.at[block])

        def body(i):
            first, at = place(block, i)
            q_block = rows_of(q_all[pl.ds(first, group)]).astype(BF16)
            s = nt_dot(q_block, keys) * factor
            m = jnp.max(s, axis=-1, keepdims=True)
            w = jnp.exp(s - m)
            total = jnp.sum(w, axis=-1, keepdims=True)
            high = w.astype(BF16)
            w_high[at] = high
            w_low[at] = (w - high.astype(F32)).astype(BF16)
            total_all[at] = total
            log_all[at] = m + jnp.log(total)

        repeat(0, groups, body)

    repeat(0, blocks, lambda b: weigh(lax.rem(mine + b, blocks)))

    settle(others(v_all), v_rs)
    values = v_all[...].reshape(kvh * tokens, dim)
    diag_row = lax.broadcasted_iota(jnp.int32, (per, 128), 0)
    diag_lane = lax.broadcasted_iota(jnp.int32, (per, 128), 1)
    at_log = diag_lane == diag_row
    at_unit = diag_lane == diag_row + 64

    def emit(block):
        def body(i):
            first, at = place(block, i)
            sums = jnp.dot(w_high[at], values, preferred_element_type=F32) + jnp.dot(
                w_low[at], values, preferred_element_type=F32
            )
            largest = jnp.maximum(jnp.max(jnp.abs(sums), axis=-1, keepdims=True), 1e-30)
            code = jnp.round(sums * (STEPS_OF_CODE / largest)).astype(jnp.int32).astype(I16)
            o_send[pl.ds(first, group)] = code.reshape(group, steps, gsize, dim)
            unit = largest / (STEPS_OF_CODE * total_all[at])
            both = jnp.where(
                at_log[None],
                jnp.broadcast_to(log_all[at], (span, 128)).reshape(group, per, 128),
                jnp.where(
                    at_unit[None],
                    jnp.broadcast_to(unit, (span, 128)).reshape(group, per, 128),
                    0.0,
                ),
            )
            l_send[pl.ds(first, group)] = jnp.sum(both, axis=1, keepdims=True)
            for j in range(group):
                dev = first + j

                @pl.when(dev != me)
                def _():
                    remote(o_send.at[dev], o_all.at[me], o_ss, o_rs.at[mine], dev).start()
                    remote(l_send.at[dev], l_all.at[me], l_ss, l_rs.at[mine], dev).start()

                @pl.when(dev == me)
                def _():
                    pltpu.make_async_copy(o_send.at[dev], o_all.at[dev], o_rs.at[mine]).start()
                    pltpu.make_async_copy(l_send.at[dev], l_all.at[dev], l_rs.at[mine]).start()

        repeat(0, groups, body)

    repeat(1, blocks + 1, lambda b: emit(lax.rem(mine + b, blocks)))

    highest, upper, lower = own_max, own_sum, own_total
    for r in range(blocks):
        part = pl.ds(r * kvh, kvh)
        settle(l_all.at[part], l_rs.at[r])
        spread = jnp.broadcast_to(l_all[part], (kvh, per, 128))

        def column(where):
            return jnp.sum(
                jnp.where(where[None], spread, 0.0), axis=-1, keepdims=True
            ).reshape(rows, 1)

        log = column(at_log)
        unit = column(at_unit)
        now = jnp.maximum(highest, log)
        keep, weight = jnp.exp(highest - now), jnp.exp(log - now)
        settle(o_all.at[part], o_rs.at[r])
        piece = o_all[part].astype(jnp.int32).astype(F32).reshape(rows, dim)
        upper = upper * keep + (weight * unit) * piece
        lower = lower * keep + weight
        highest = now
    result = upper / lower
    for h in range(kvh):
        for t in range(steps):
            at = h * per + t * gsize
            out_ref[t, h] = result[at:at + gsize]

    settle(q_all.at[pl.ds(0, n - 1)], q_ss)
    settle(others(k_all), k_ss)
    settle(others(v_all), v_ss)
    settle(o_all.at[pl.ds(0, n - 1)], o_ss)
    settle(l_all.at[pl.ds(0, n - 1)], l_ss)


def solution(mesh):
    n = mesh.shape["sample"]

    def shards(queries, pk, pv, sk, sv, lengths, nk, nv):
        _, steps, heads, dim = queries.shape
        tokens, kvh, _ = pk.shape
        gsize = heads // kvh
        suffix = sk.shape[1]
        per = steps * gsize
        group = math.gcd(kvh, 4)
        chunk = math.gcd(suffix * kvh, 1024)
        chunks = suffix * kvh // chunk
        dma = pltpu.SemaphoreType.DMA
        out = pl.pallas_call(
            functools.partial(kernel, n, group, chunk),
            out_shape=jax.ShapeDtypeStruct((steps, kvh, gsize, dim), F32),
            in_specs=[pl.BlockSpec(memory_space=pltpu.SMEM)]
            + [pl.BlockSpec(memory_space=pltpu.HBM)] * 7,
            out_specs=pl.BlockSpec(memory_space=pltpu.VMEM),
            scratch_shapes=[
                pltpu.VMEM((steps, kvh, gsize, dim), BF16),
                pltpu.VMEM((tokens * kvh, dim), BF16),
                pltpu.VMEM((tokens * kvh, dim), BF16),
                pltpu.VMEM((tokens * kvh, dim), F32),
                pltpu.VMEM((kvh, tokens, dim), BF16),
                pltpu.VMEM((kvh, tokens, dim), BF16),
                pltpu.VMEM((n, steps, gsize, dim), BF16),
                pltpu.VMEM((kvh, tokens, dim), BF16),
                pltpu.VMEM((kvh, tokens, dim), BF16),
                pltpu.VMEM((suffix * kvh, dim), BF16),
                pltpu.VMEM((suffix * kvh, dim), BF16),
                pltpu.VMEM((steps, kvh, dim), BF16),
                pltpu.VMEM((steps, kvh, dim), BF16),
                pltpu.VMEM((chunks, kvh * per, chunk), F32),
                pltpu.VMEM((n, steps, gsize, dim), I16),
                pltpu.VMEM((n, 1, 128), F32),
                pltpu.VMEM((n, steps, gsize, dim), I16),
                pltpu.VMEM((n, 1, 128), F32),
                pltpu.VMEM((n * per, kvh * tokens), BF16),
                pltpu.VMEM((n * per, kvh * tokens), BF16),
                pltpu.VMEM((n * per, 1), F32),
                pltpu.VMEM((n * per, 1), F32),
                dma((5,)), dma((2 * chunks,)), pltpu.SemaphoreType.REGULAR,
                dma, dma((n // kvh,)), dma, dma, dma, dma,
                dma, dma((n // kvh,)), dma, dma((n // kvh,)),
            ],
            compiler_params=pltpu.CompilerParams(
                collective_id=0, has_side_effects=True, vmem_limit_bytes=48 << 20
            ),
        )(lengths, *[pltpu.with_memory_space_constraint(x, pltpu.HBM) for x in (
            queries.reshape(steps, kvh, gsize, dim),
            pk.reshape(tokens * kvh, dim),
            pv.reshape(tokens * kvh, dim),
            sk.reshape(suffix * kvh, dim),
            sv.reshape(suffix * kvh, dim),
            nk.reshape(steps, kvh, dim),
            nv.reshape(steps, kvh, dim),
        )])
        return out.reshape(1, steps, heads, dim)

    spread = ("group", "sample")
    four = P(spread, None, None, None)
    three = P(spread, None, None)
    return jax.shard_map(
        shards, mesh=mesh,
        in_specs=(four, three, three, four, four, P(spread), four, four),
        out_specs=four, check_vma=False,
    )
```

time: 23.2 us -> 21.3 us (0.918)
  Pallas kernels: 21.8 us -> 19.8 us
    pallas_call x1, Pallas kernels: 21.8 us -> 19.8 us  [shards(): pl.pallas_call(functools.partial(kernel, n, group, chunk), out_shape=jax....]
where the time goes in v1:
time: 21.3 us; the launch traced here: 21.1 us
  Pallas kernels  19.8 us (93%)
  between operations  0.66 us (3%)
  local copies, waits for them, and re-layouts  0.64 us (3%)
    pallas_call x1, Pallas kernels, shards(): pl.pallas_call(functools.partial(kernel, n, group, chunk), out_shape=jax....  19.8 us
    unnamed x1, local copies, waits for them, and re-layouts  0.64 us

profile of v1, /device:TPU:0, one launch (start us, length us, event | category | flops | bytes accessed | tf_op | source)
XLA Modules:
  0.0 21.1 jit_solution(13802333773944097122)
XLA Ops:
  0.7 19.8 %shard_map.82 = f32[3,8,8,128]{3,2,1,0:T(8,128)S(1)} custom-call(s32[1]{0:T(128)S(6)} %copy.10.lens, bf16[3,8,8,128]{3,2,1,0:T(8,128)(2,1)} %bitcast.13, bf16[1024,128]{1,0:T(8,128)(2,1)} %bitcast.11, bf16[1024,128]{1,0:T(8,128)(2,1)} %bitcast.12, bf16[8192,128]{1,0:T(8,128)(2,1)} %bitcast.9, bf16[8192,128]{1,0:T(8,128)(2,1)} %bitcast.10, ...), custom_call_target="tpu_custom_call" | custom-call | tf_op jit(solution)/shard_map/pallas_call | solution.py:307
  20.5 0.6 %copy.11 = f32[1,3,64,128]{3,2,1,0:T(8,128)} copy(f32[1,3,64,128]{3,2,1,0:T(8,128)S(1)} %bitcast.8) | data formatting | bytes 196608

commit v2 on v1

--- a/solution.py
+++ b/solution.py
@@ -27,7 +27,7 @@
     out_ref,
     q_own, pk, pv, wide, k_send, v_send, q_all, k_all, v_all, sk, sv, nk, nv, s_own,
     o_send, l_send, o_all, l_all, w_high, w_low, log_all, total_all,
-    local_sem, suf_sem, block_sem, q_ss, q_rs, k_ss, k_rs, v_ss, v_rs, o_ss, o_rs, l_ss, l_rs,
+    local_sem, suf_sem, late_sem, block_sem, q_ss, q_rs, k_ss, k_rs, v_ss, v_rs, o_ss, o_rs, l_ss, l_rs,
 ):
     steps, kvh, gsize, dim = q_hbm.shape
     per = steps * gsize
@@ -57,26 +57,41 @@
             return 0
         lax.fori_loop(first, last, body, 0)
 
-    barrier = pltpu.get_barrier_semaphore()
-    paired = blocks == 2
-    second = base > 0
-    other = lax.rem(base + kvh, n)
-    if paired:
-        repeat(1, kvh, lambda d: signal(barrier, base + lax.rem(head + d, kvh)))
-
-        @pl.when(jnp.logical_not(second))
-        def _():
-            repeat(0, kvh, lambda d: signal(barrier, other + lax.rem(head + d, kvh)))
-    else:
-        repeat(1, n, lambda d: signal(barrier, lax.rem(me + d, n)))
-
     local = [
         pltpu.make_async_copy(a, b, local_sem.at[i])
         for i, (a, b) in enumerate(
             [(pk_hbm, pk), (pv_hbm, pv), (q_hbm, q_own), (nk_hbm, nk), (nv_hbm, nv)]
         )
     ]
-    for c in local:
+    local[0].start()
+
+    barrier = pltpu.get_barrier_semaphore()
+    paired = blocks == 2 and kvh % 2 == 0 and kvh >= 4
+    second = base > 0
+    other = lax.rem(base + kvh, n)
+    early = kvh - 2 if paired else kvh
+    late = head >= early
+
+    def to_early(action):
+        repeat(jnp.where(late, 0, 1), early, lambda d: action(lax.rem(head + d, early)))
+
+    def to_late(action):
+        if paired:
+            repeat(
+                0, jnp.where(late, 1, 2), lambda d: action(early + lax.rem(head + 1 + d, 2))
+            )
+
+    def unless(skipped, action):
+        pl.when(jnp.logical_not(skipped))(action)
+
+    if paired:
+        unless(late, lambda: to_early(lambda hd: signal(barrier, base + hd)))
+        to_late(lambda hd: signal(barrier, base + hd))
+        unless(second, lambda: repeat(early, kvh, lambda hd: signal(barrier, other + hd)))
+    else:
+        repeat(1, n, lambda d: signal(barrier, lax.rem(me + d, n)))
+
+    for c in local[1:]:
         c.start()
     own_q = pltpu.make_async_copy(q_hbm.at[:, head], q_all.at[me], q_rs.at[mine])
     own_q.start()
@@ -100,42 +115,51 @@
     def send_q(dev):
         remote(q_hbm.at[:, lax.rem(dev, kvh)], q_all.at[me], q_ss, q_rs.at[mine], dev).start()
 
-    def send_kv(d, src, dst, ss, rs):
-        hd = lax.rem(head + d, kvh)
-        remote(src.at[hd], dst.at[head], ss, rs, base + hd).start()
-
-    def near_q(d):
-        send_q(base + lax.rem(head + d, kvh))
-
-    def far_q(d):
-        send_q(lax.rem(base + kvh + lax.rem(head + d, kvh) + lax.div(d, kvh) * kvh, n))
-
-    def all_far_q():
-        repeat(0, n - kvh, far_q)
+    def send_k(hd):
+        remote(k_send.at[hd], k_all.at[head], k_ss, k_rs, base + hd).start()
+
+    def send_v(hd):
+        remote(v_send.at[hd], v_all.at[head], v_ss, v_rs, base + hd).start()
+
+    def near_q(hd):
+        send_q(base + hd)
+
+    def far_q():
+        repeat(0, n - kvh, lambda d: send_q(
+            lax.rem(base + kvh + lax.rem(head + d, kvh) + lax.div(d, kvh) * kvh, n)
+        ))
 
     if paired:
-        @pl.when(second)
+        @pl.when(late)
         def _():
-            pl.semaphore_wait(barrier, n - 1)
-            repeat(0, kvh, lambda d: signal(block_sem, other + lax.rem(head + d, kvh)))
-            all_far_q()
-
-        @pl.when(jnp.logical_not(second))
-        def _():
-            pl.semaphore_wait(barrier, kvh - 1)
+            pl.semaphore_wait(barrier, jnp.where(second, n - 1, kvh - 1))
+            repeat(0, early, lambda hd: signal(late_sem, base + hd))
+
+            @pl.when(second)
+            def _():
+                repeat(0, kvh // 2, lambda d: signal(block_sem, other + 2 * d + head - early))
+
+        unless(late, lambda: pl.semaphore_wait(barrier, early - 1))
     else:
         pl.semaphore_wait(barrier, n - 1)
-        all_far_q()
-    repeat(1, kvh, near_q)
+    to_early(near_q)
     split(pk, local[0], k_send, k_all)
-    repeat(1, kvh, lambda d: send_kv(d, k_send, k_all, k_ss, k_rs))
+    to_early(send_k)
+    if paired:
+        unless(late, lambda: pl.semaphore_wait(late_sem, 2))
+        to_late(near_q)
+        to_late(send_k)
+        pl.when(second)(far_q)
+    else:
+        far_q()
     split(pv, local[1], v_send, v_all)
     if paired:
         @pl.when(jnp.logical_not(second))
         def _():
-            pl.semaphore_wait(block_sem, kvh)
-            all_far_q()
-    repeat(1, kvh, lambda d: send_kv(d, v_send, v_all, v_ss, v_rs))
+            pl.semaphore_wait(block_sem, 1)
+            far_q()
+    to_early(send_v)
+    to_late(send_v)
 
     for c in local[2:]:
         c.wait()
@@ -333,7 +357,8 @@
                 pltpu.VMEM((n * per, kvh * tokens), BF16),
                 pltpu.VMEM((n * per, 1), F32),
                 pltpu.VMEM((n * per, 1), F32),
-                dma((5,)), dma((2 * chunks,)), pltpu.SemaphoreType.REGULAR,
+                dma((5,)), dma((2 * chunks,)),
+                pltpu.SemaphoreType.REGULAR, pltpu.SemaphoreType.REGULAR,
                 dma, dma((n // kvh,)), dma, dma, dma, dma,
                 dma, dma((n // kvh,)), dma, dma((n // kvh,)),
             ],

time: 21.3 us -> 20.7 us (0.972)
  Pallas kernels: 19.8 us -> 19.2 us
    pallas_call x1, Pallas kernels: 19.8 us -> 19.2 us  [shards(): pl.pallas_call(functools.partial(kernel, n, group, chunk), out_shape=jax....]
where the time goes in v2:
time: 20.7 us; the launch traced here: 20.6 us
  Pallas kernels  19.2 us (93%)
  between operations  0.66 us (3%)
  local copies, waits for them, and re-layouts  0.64 us (3%)
    pallas_call x1, Pallas kernels, shards(): pl.pallas_call(functools.partial(kernel, n, group, chunk), out_shape=jax....  19.2 us
    unnamed x1, local copies, waits for them, and re-layouts  0.64 us

profile of v2, /device:TPU:0, one launch (start us, length us, event | category | flops | bytes accessed | tf_op | source)
XLA Modules:
  0.0 20.6 jit_solution(10731272065533598234)
XLA Ops:
  0.7 19.2 %shard_map.82 = f32[3,8,8,128]{3,2,1,0:T(8,128)S(1)} custom-call(s32[1]{0:T(128)S(6)} %copy.10.lens, bf16[3,8,8,128]{3,2,1,0:T(8,128)(2,1)} %bitcast.13, bf16[1024,128]{1,0:T(8,128)(2,1)} %bitcast.11, bf16[1024,128]{1,0:T(8,128)(2,1)} %bitcast.12, bf16[8192,128]{1,0:T(8,128)(2,1)} %bitcast.9, bf16[8192,128]{1,0:T(8,128)(2,1)} %bitcast.10, ...), custom_call_target="tpu_custom_call" | custom-call | tf_op jit(solution)/shard_map/pallas_call | solution.py:331
  19.9 0.6 %copy.11 = f32[1,3,64,128]{3,2,1,0:T(8,128)} copy(f32[1,3,64,128]{3,2,1,0:T(8,128)S(1)} %bitcast.8) | data formatting | bytes 196608

commit v3 on v2

--- a/solution.py
+++ b/solution.py
@@ -9,7 +9,8 @@
 from jax.sharding import PartitionSpec as P
 
 F32, BF16, I16 = jnp.float32, jnp.bfloat16, jnp.int16
-STEPS_OF_CODE = 32767.0
+CODES = 32767.0
+PARTS = 65535.0
 
 
 def rows_of(tiles):
@@ -26,8 +27,8 @@
     lens, q_hbm, pk_hbm, pv_hbm, sk_hbm, sv_hbm, nk_hbm, nv_hbm,
     out_ref,
     q_own, pk, pv, wide, k_send, v_send, q_all, k_all, v_all, sk, sv, nk, nv, s_own,
-    o_send, l_send, o_all, l_all, w_high, w_low, log_all, total_all,
-    local_sem, suf_sem, late_sem, block_sem, q_ss, q_rs, k_ss, k_rs, v_ss, v_rs, o_ss, o_rs, l_ss, l_rs,
+    o_send, o_all, w_high, w_low, log_all, total_all,
+    local_sem, suf_sem, late_sem, block_sem, q_ss, q_rs, k_ss, k_rs, v_ss, v_rs, o_ss, o_rs,
 ):
     steps, kvh, gsize, dim = q_hbm.shape
     per = steps * gsize
@@ -224,15 +225,15 @@
         def body(i):
             first, at = place(block, i)
             q_block = rows_of(q_all[pl.ds(first, group)]).astype(BF16)
-            s = nt_dot(q_block, keys) * factor
+            s = nt_dot(q_block, keys)
             m = jnp.max(s, axis=-1, keepdims=True)
-            w = jnp.exp(s - m)
+            w = jnp.exp2((s - m) * (factor * math.log2(math.e)))
             total = jnp.sum(w, axis=-1, keepdims=True)
             high = w.astype(BF16)
             w_high[at] = high
             w_low[at] = (w - high.astype(F32)).astype(BF16)
             total_all[at] = total
-            log_all[at] = m + jnp.log(total)
+            log_all[at] = m * factor + jnp.log(total)
 
         repeat(0, groups, body)
 
@@ -242,8 +243,10 @@
     values = v_all[...].reshape(kvh * tokens, dim)
     diag_row = lax.broadcasted_iota(jnp.int32, (per, 128), 0)
     diag_lane = lax.broadcasted_iota(jnp.int32, (per, 128), 1)
-    at_log = diag_lane == diag_row
-    at_unit = diag_lane == diag_row + 64
+    at_whole = diag_lane == diag_row
+    at_part = diag_lane == diag_row + 32
+    at_power = diag_lane == diag_row + 64
+    pairs = per // 2
 
     def emit(block):
         def body(i):
@@ -251,54 +254,55 @@
             sums = jnp.dot(w_high[at], values, preferred_element_type=F32) + jnp.dot(
                 w_low[at], values, preferred_element_type=F32
             )
-            largest = jnp.maximum(jnp.max(jnp.abs(sums), axis=-1, keepdims=True), 1e-30)
-            code = jnp.round(sums * (STEPS_OF_CODE / largest)).astype(jnp.int32).astype(I16)
-            o_send[pl.ds(first, group)] = code.reshape(group, steps, gsize, dim)
-            unit = largest / (STEPS_OF_CODE * total_all[at])
-            both = jnp.where(
-                at_log[None],
-                jnp.broadcast_to(log_all[at], (span, 128)).reshape(group, per, 128),
-                jnp.where(
-                    at_unit[None],
-                    jnp.broadcast_to(unit, (span, 128)).reshape(group, per, 128),
-                    0.0,
-                ),
-            )
-            l_send[pl.ds(first, group)] = jnp.sum(both, axis=1, keepdims=True)
+            total = total_all[at]
+            largest = jnp.max(jnp.abs(sums), axis=-1, keepdims=True)
+            power = jnp.ceil(jnp.log2(jnp.maximum(largest / total, 1e-30)))
+            code = jnp.round(sums * (CODES * jnp.exp2(-power) / total))
+            log = log_all[at]
+            whole = jnp.floor(log)
+            part = jnp.round((log - whole) * PARTS) - 32768.0
+
+            def lanes(column):
+                return jnp.broadcast_to(column, (span, 128)).reshape(group, per, 128)
+
+            facts = jnp.where(at_whole[None], lanes(whole), jnp.where(
+                at_part[None], lanes(part), jnp.where(at_power[None], lanes(power), 0.0)
+            ))
+            facts = jnp.broadcast_to(jnp.sum(facts, axis=1, keepdims=True), (group, 2, 128))
+            here = pl.ds(first, group)
+            o_send[here, 0:pairs] = code.astype(jnp.int32).astype(I16).reshape(group, pairs, 2, dim)
+            o_send[here, pairs:] = facts.astype(jnp.int32).astype(I16).reshape(group, 1, 2, dim)
             for j in range(group):
                 dev = first + j
 
                 @pl.when(dev != me)
                 def _():
                     remote(o_send.at[dev], o_all.at[me], o_ss, o_rs.at[mine], dev).start()
-                    remote(l_send.at[dev], l_all.at[me], l_ss, l_rs.at[mine], dev).start()
 
                 @pl.when(dev == me)
                 def _():
                     pltpu.make_async_copy(o_send.at[dev], o_all.at[dev], o_rs.at[mine]).start()
-                    pltpu.make_async_copy(l_send.at[dev], l_all.at[dev], l_rs.at[mine]).start()
 
         repeat(0, groups, body)
 
     repeat(1, blocks + 1, lambda b: emit(lax.rem(mine + b, blocks)))
 
+    log_scales = jnp.where(at_whole, 1.0, jnp.where(at_part, 1.0 / PARTS, 0.0))
     highest, upper, lower = own_max, own_sum, own_total
     for r in range(blocks):
         part = pl.ds(r * kvh, kvh)
-        settle(l_all.at[part], l_rs.at[r])
-        spread = jnp.broadcast_to(l_all[part], (kvh, per, 128))
-
-        def column(where):
-            return jnp.sum(
-                jnp.where(where[None], spread, 0.0), axis=-1, keepdims=True
-            ).reshape(rows, 1)
-
-        log = column(at_log)
-        unit = column(at_unit)
+        settle(o_all.at[part], o_rs.at[r])
+        facts = o_all[part, pairs:].astype(jnp.int32).astype(F32)
+        spread = jnp.broadcast_to(facts.reshape(kvh, 2, 128)[:, 0:1], (kvh, per, 128))
+
+        def column(scales):
+            return jnp.sum(spread * scales[None], axis=-1, keepdims=True).reshape(rows, 1)
+
+        log = column(log_scales) + 32768.0 / PARTS
+        unit = jnp.exp2(column(jnp.where(at_power, 1.0, 0.0))) * (1.0 / CODES)
         now = jnp.maximum(highest, log)
         keep, weight = jnp.exp(highest - now), jnp.exp(log - now)
-        settle(o_all.at[part], o_rs.at[r])
-        piece = o_all[part].astype(jnp.int32).astype(F32).reshape(rows, dim)
+        piece = o_all[part, 0:pairs].astype(jnp.int32).astype(F32).reshape(rows, dim)
         upper = upper * keep + (weight * unit) * piece
         lower = lower * keep + weight
         highest = now
@@ -312,7 +316,6 @@
     settle(others(k_all), k_ss)
     settle(others(v_all), v_ss)
     settle(o_all.at[pl.ds(0, n - 1)], o_ss)
-    settle(l_all.at[pl.ds(0, n - 1)], l_ss)
 
 
 def solution(mesh):
@@ -349,10 +352,8 @@
                 pltpu.VMEM((steps, kvh, dim), BF16),
                 pltpu.VMEM((steps, kvh, dim), BF16),
                 pltpu.VMEM((chunks, kvh * per, chunk), F32),
-                pltpu.VMEM((n, steps, gsize, dim), I16),
-                pltpu.VMEM((n, 1, 128), F32),
-                pltpu.VMEM((n, steps, gsize, dim), I16),
-                pltpu.VMEM((n, 1, 128), F32),
+                pltpu.VMEM((n, per // 2 + 1, 2, dim), I16),
+                pltpu.VMEM((n, per // 2 + 1, 2, dim), I16),
                 pltpu.VMEM((n * per, kvh * tokens), BF16),
                 pltpu.VMEM((n * per, kvh * tokens), BF16),
                 pltpu.VMEM((n * per, 1), F32),
@@ -360,7 +361,7 @@
                 dma((5,)), dma((2 * chunks,)),
                 pltpu.SemaphoreType.REGULAR, pltpu.SemaphoreType.REGULAR,
                 dma, dma((n // kvh,)), dma, dma, dma, dma,
-                dma, dma((n // kvh,)), dma, dma((n // kvh,)),
+                dma, dma((n // kvh,)),
             ],
             compiler_params=pltpu.CompilerParams(
                 collective_id=0, has_side_effects=True, vmem_limit_bytes=48 << 20

time: 20.7 us -> 20.6 us (level)
  no operation moved by 1% of the time
where the time goes in v3:
time: 20.6 us; the launch traced here: 20.5 us
  Pallas kernels  19.2 us (93%)
  between operations  0.66 us (3%)
  local copies, waits for them, and re-layouts  0.64 us (3%)
    pallas_call x1, Pallas kernels, shards(): pl.pallas_call(functools.partial(kernel, n, group, chunk), out_shape=jax....  19.2 us
    unnamed x1, local copies, waits for them, and re-layouts  0.64 us

profile of v3, /device:TPU:0, one launch (start us, length us, event | category | flops | bytes accessed | tf_op | source)
XLA Modules:
  0.0 20.5 jit_solution(1743065940293401755)
XLA Ops:
  0.7 19.2 %shard_map.82 = f32[3,8,8,128]{3,2,1,0:T(8,128)S(1)} custom-call(s32[1]{0:T(128)S(6)} %copy.10.lens, bf16[3,8,8,128]{3,2,1,0:T(8,128)(2,1)} %bitcast.13, bf16[1024,128]{1,0:T(8,128)(2,1)} %bitcast.11, bf16[1024,128]{1,0:T(8,128)(2,1)} %bitcast.12, bf16[8192,128]{1,0:T(8,128)(2,1)} %bitcast.9, bf16[8192,128]{1,0:T(8,128)(2,1)} %bitcast.10, ...), custom_call_target="tpu_custom_call" | custom-call | tf_op jit(solution)/shard_map/pallas_call | solution.py:334
  19.8 0.6 %copy.11 = f32[1,3,64,128]{3,2,1,0:T(8,128)} copy(f32[1,3,64,128]{3,2,1,0:T(8,128)S(1)} %bitcast.8) | data formatting | bytes 196608

commit v4 on v3

--- a/solution.py
+++ b/solution.py
@@ -23,12 +23,12 @@
 
 
 def kernel(
-    n, group, chunk,
+    n, group,
     lens, q_hbm, pk_hbm, pv_hbm, sk_hbm, sv_hbm, nk_hbm, nv_hbm,
     out_ref,
-    q_own, pk, pv, wide, k_send, v_send, q_all, k_all, v_all, sk, sv, nk, nv, s_own,
+    q_own, relay, pk, pv, wide, k_send, v_send, q_all, k_all, v_all, sk, sv, nk, nv, s_own, hide,
     o_send, o_all, w_high, w_low, log_all, total_all,
-    local_sem, suf_sem, late_sem, block_sem, q_ss, q_rs, k_ss, k_rs, v_ss, v_rs, o_ss, o_rs,
+    local_sem, suf_sem, late_sem, block_sem, relay_ss, relay_rs, q_ss, q_rs, k_ss, k_rs, v_ss, v_rs, o_ss, o_rs,
 ):
     steps, kvh, gsize, dim = q_hbm.shape
     per = steps * gsize
@@ -38,7 +38,7 @@
     head = lax.rem(me, kvh)
     mine = lax.div(me, kvh)
     base = me - head
-    chunks = sk.shape[0] // chunk
+    couples, suffix = sk.shape[:2]
     blocks = n // kvh
 
     def remote(src, dst, ss, rs, dev):
@@ -65,6 +65,7 @@
         )
     ]
     local[0].start()
+    local[1].start()
 
     barrier = pltpu.get_barrier_semaphore()
     paired = blocks == 2 and kvh % 2 == 0 and kvh >= 4
@@ -92,20 +93,6 @@
     else:
         repeat(1, n, lambda d: signal(barrier, lax.rem(me + d, n)))
 
-    for c in local[1:]:
-        c.start()
-    own_q = pltpu.make_async_copy(q_hbm.at[:, head], q_all.at[me], q_rs.at[mine])
-    own_q.start()
-    halves = []
-    for i, (a, b) in enumerate([(sk_hbm, sk), (sv_hbm, sv)]):
-        for c in range(chunks):
-            part = pl.ds(c * chunk, chunk)
-            halves.append(
-                pltpu.make_async_copy(a.at[part], b.at[part], suf_sem.at[i * chunks + c])
-            )
-    for c in halves:
-        c.start()
-
     def split(src, copy, dst, kept):
         copy.wait()
         wide[...] = src[...].astype(F32)
@@ -113,6 +100,12 @@
             dst[h] = wide[pl.ds(h, tokens, stride=kvh), :].astype(BF16)
         kept[head] = wide[pl.ds(head, tokens, stride=kvh), :].astype(BF16)
 
+    def settle(ref, sem):
+        pltpu.make_async_copy(ref, ref, sem).wait()
+
+    def others(ref):
+        return ref.at[pl.ds(0, kvh - 1)]
+
     def send_q(dev):
         remote(q_hbm.at[:, lax.rem(dev, kvh)], q_all.at[me], q_ss, q_rs.at[mine], dev).start()
 
@@ -130,6 +123,26 @@
             lax.rem(base + kvh + lax.rem(head + d, kvh) + lax.div(d, kvh) * kvh, n)
         ))
 
+    half = kvh // 2
+    outer = jnp.logical_not(second) & (head < half)
+    inner = jnp.logical_not(second) & (head >= half)
+    passes_to = lax.rem(head + half, kvh)
+    must_ask = passes_to >= early
+
+    def hand_over():
+        remote(q_hbm, relay, q_ss, relay_rs, base + passes_to).start()
+
+    def pass_on():
+        settle(relay, relay_rs)
+
+        def forward(d):
+            hd = lax.rem(head + d, kvh)
+            remote(
+                relay.at[:, hd], q_all.at[base + passes_to], relay_ss, q_rs.at[mine], other + hd
+            ).start()
+
+        repeat(0, kvh, forward)
+
     if paired:
         @pl.when(late)
         def _():
@@ -143,24 +156,37 @@
         unless(late, lambda: pl.semaphore_wait(barrier, early - 1))
     else:
         pl.semaphore_wait(barrier, n - 1)
+    if paired:
+        pl.when(outer & jnp.logical_not(must_ask))(hand_over)
     to_early(near_q)
     split(pk, local[0], k_send, k_all)
     to_early(send_k)
+    for c in local[2:]:
+        c.start()
+    own_q = pltpu.make_async_copy(q_hbm.at[:, head], q_all.at[me], q_rs.at[mine])
+    own_q.start()
+    halves = [
+        pltpu.make_async_copy(a.at[:, c], b.at[c], suf_sem.at[i * couples + c])
+        for i, (a, b) in enumerate([(sk_hbm, sk), (sv_hbm, sv)]) for c in range(couples)
+    ]
+    for c in halves:
+        c.start()
     if paired:
         unless(late, lambda: pl.semaphore_wait(late_sem, 2))
+        pl.when(outer & must_ask)(hand_over)
         to_late(near_q)
         to_late(send_k)
         pl.when(second)(far_q)
     else:
         far_q()
     split(pv, local[1], v_send, v_all)
+    to_early(send_v)
+    to_late(send_v)
     if paired:
         @pl.when(jnp.logical_not(second))
         def _():
             pl.semaphore_wait(block_sem, 1)
-            far_q()
-    to_early(send_v)
-    to_late(send_v)
+            pl.when(inner)(far_q)
 
     for c in local[2:]:
         c.wait()
@@ -174,18 +200,22 @@
     lane_head = lax.rem(lane, kvh)
     match = (row >= lane_head * per) & (row < (lane_head + 1) * per)
     bias = jnp.where(match, 0.0, -jnp.inf).astype(F32)
-    bias_wide = jnp.concatenate([bias] * (chunk // 128), axis=1)
-    token_of = lax.div(lax.broadcasted_iota(jnp.int32, (8, chunk), 1), kvh)
-
-    top = jnp.full((rows, 1), -jnp.inf, F32)
-    for c in range(chunks):
+    two = rows // couples
+    key = lax.broadcasted_iota(jnp.int32, (two, 2 * suffix), 1)
+    wide_row = lax.broadcasted_iota(jnp.int32, (two, 2 * suffix), 0)
+    seen = (lax.rem(key, 2) == lax.div(wide_row, per)) & (lax.div(key, 2) < length)
+    hide[...] = jnp.where(seen, 0.0, -jnp.inf).astype(F32)
+
+    tops = []
+    for c in range(couples):
         halves[c].wait()
-        s = nt_dot(q_rows, sk[c * chunk:(c + 1) * chunk, :]) * factor
-        limit = jnp.where(token_of < length - c * (chunk // kvh), 0.0, -jnp.inf).astype(F32)[:1]
-        s = s + bias_wide + limit
+        s = nt_dot(q_rows[c * two:(c + 1) * two], sk[c].reshape(2 * suffix, dim)) * factor + hide[...]
         s_own[c] = s
-        top = jnp.maximum(top, jnp.max(s, axis=-1, keepdims=True))
-
+        tops.append(jnp.max(s, axis=-1, keepdims=True))
+    top = jnp.concatenate(tops, axis=0)
+
+    if paired:
+        pl.when(inner)(pass_on)
     pad = jnp.zeros((128 - steps * kvh, dim), F32)
     new_k = jnp.concatenate([nk[j].astype(F32) for j in range(steps)] + [pad], axis=0).astype(BF16)
     new_v = jnp.concatenate([nv[j].astype(F32) for j in range(steps)] + [pad], axis=0).astype(BF16)
@@ -196,19 +226,16 @@
     w_new = jnp.exp(s_new - own_max)
     own_total = jnp.sum(w_new, axis=-1, keepdims=True)
     own_sum = jnp.dot(w_new.astype(BF16), new_v, preferred_element_type=F32)
-    for c in range(chunks):
-        halves[chunks + c].wait()
-        w = jnp.exp(s_own[c] - own_max)
-        own_total = own_total + jnp.sum(w, axis=-1, keepdims=True)
-        own_sum = own_sum + jnp.dot(
-            w.astype(BF16), sv[c * chunk:(c + 1) * chunk, :], preferred_element_type=F32
-        )
-
-    def settle(ref, sem):
-        pltpu.make_async_copy(ref, ref, sem).wait()
-
-    def others(ref):
-        return ref.at[pl.ds(0, kvh - 1)]
+    totals, sums_of = [], []
+    for c in range(couples):
+        halves[couples + c].wait()
+        w = jnp.exp(s_own[c] - own_max[c * two:(c + 1) * two])
+        totals.append(jnp.sum(w, axis=-1, keepdims=True))
+        sums_of.append(jnp.dot(
+            w.astype(BF16), sv[c].reshape(2 * suffix, dim), preferred_element_type=F32
+        ))
+    own_total = own_total + jnp.concatenate(totals, axis=0)
+    own_sum = own_sum + jnp.concatenate(sums_of, axis=0)
 
     settle(others(k_all), k_rs)
     keys = k_all[...].reshape(kvh * tokens, dim)
@@ -222,9 +249,10 @@
     def weigh(block):
         settle(q_all.at[pl.ds(block * kvh, kvh)], q_rs.at[block])
 
-        def body(i):
-            first, at = place(block, i)
-            q_block = rows_of(q_all[pl.ds(first, group)]).astype(BF16)
+        if True:
+            first = block * kvh
+            at = pl.ds(pl.multiple_of(first * per, kvh * per), kvh * per)
+            q_block = rows_of(q_all[pl.ds(first, kvh)]).astype(BF16)
             s = nt_dot(q_block, keys)
             m = jnp.max(s, axis=-1, keepdims=True)
             w = jnp.exp2((s - m) * (factor * math.log2(math.e)))
@@ -235,7 +263,6 @@
             total_all[at] = total
             log_all[at] = m * factor + jnp.log(total)
 
-        repeat(0, groups, body)
 
     repeat(0, blocks, lambda b: weigh(lax.rem(mine + b, blocks)))
 
@@ -313,6 +340,8 @@
             out_ref[t, h] = result[at:at + gsize]
 
     settle(q_all.at[pl.ds(0, n - 1)], q_ss)
+    if paired:
+        pl.when(inner)(lambda: settle(q_all.at[pl.ds(0, kvh)], relay_ss))
     settle(others(k_all), k_ss)
     settle(others(v_all), v_ss)
     settle(o_all.at[pl.ds(0, n - 1)], o_ss)
@@ -328,16 +357,15 @@
         suffix = sk.shape[1]
         per = steps * gsize
         group = math.gcd(kvh, 4)
-        chunk = math.gcd(suffix * kvh, 1024)
-        chunks = suffix * kvh // chunk
         dma = pltpu.SemaphoreType.DMA
         out = pl.pallas_call(
-            functools.partial(kernel, n, group, chunk),
+            functools.partial(kernel, n, group),
             out_shape=jax.ShapeDtypeStruct((steps, kvh, gsize, dim), F32),
             in_specs=[pl.BlockSpec(memory_space=pltpu.SMEM)]
             + [pl.BlockSpec(memory_space=pltpu.HBM)] * 7,
             out_specs=pl.BlockSpec(memory_space=pltpu.VMEM),
             scratch_shapes=[
+                pltpu.VMEM((steps, kvh, gsize, dim), BF16),
                 pltpu.VMEM((steps, kvh, gsize, dim), BF16),
                 pltpu.VMEM((tokens * kvh, dim), BF16),
                 pltpu.VMEM((tokens * kvh, dim), BF16),
@@ -347,19 +375,20 @@
                 pltpu.VMEM((n, steps, gsize, dim), BF16),
                 pltpu.VMEM((kvh, tokens, dim), BF16),
                 pltpu.VMEM((kvh, tokens, dim), BF16),
-                pltpu.VMEM((suffix * kvh, dim), BF16),
-                pltpu.VMEM((suffix * kvh, dim), BF16),
+                pltpu.VMEM((kvh // 2, suffix, 2, dim), BF16),
+                pltpu.VMEM((kvh // 2, suffix, 2, dim), BF16),
                 pltpu.VMEM((steps, kvh, dim), BF16),
                 pltpu.VMEM((steps, kvh, dim), BF16),
-                pltpu.VMEM((chunks, kvh * per, chunk), F32),
+                pltpu.VMEM((kvh // 2, 2 * per, 2 * suffix), F32),
+                pltpu.VMEM((2 * per, 2 * suffix), F32),
                 pltpu.VMEM((n, per // 2 + 1, 2, dim), I16),
                 pltpu.VMEM((n, per // 2 + 1, 2, dim), I16),
                 pltpu.VMEM((n * per, kvh * tokens), BF16),
                 pltpu.VMEM((n * per, kvh * tokens), BF16),
                 pltpu.VMEM((n * per, 1), F32),
                 pltpu.VMEM((n * per, 1), F32),
-                dma((5,)), dma((2 * chunks,)),
-                pltpu.SemaphoreType.REGULAR, pltpu.SemaphoreType.REGULAR,
+                dma((5,)), dma((kvh,)),
+                pltpu.SemaphoreType.REGULAR, pltpu.SemaphoreType.REGULAR, dma, dma,
                 dma, dma((n // kvh,)), dma, dma, dma, dma,
                 dma, dma((n // kvh,)),
             ],
@@ -370,8 +399,8 @@
             queries.reshape(steps, kvh, gsize, dim),
             pk.reshape(tokens * kvh, dim),
             pv.reshape(tokens * kvh, dim),
-            sk.reshape(suffix * kvh, dim),
-            sv.reshape(suffix * kvh, dim),
+            sk.reshape(suffix, kvh // 2, 2, dim),
+            sv.reshape(suffix, kvh // 2, 2, dim),
             nk.reshape(steps, kvh, dim),
             nv.reshape(steps, kvh, dim),
         )])

time: 20.6 us -> 20.7 us (level)
  no operation moved by 1% of the time
where the time goes in v4:
time: 20.7 us; the launch traced here: 20.5 us
  Pallas kernels  19.2 us (93%)
  between operations  0.66 us (3%)
  local copies, waits for them, and re-layouts  0.64 us (3%)
    pallas_call x1, Pallas kernels, shards(): pl.pallas_call(functools.partial(kernel, n, group), out_shape=jax.ShapeDt...  19.2 us
    unnamed x1, local copies, waits for them, and re-layouts  0.64 us

profile of v4, /device:TPU:0, one launch (start us, length us, event | category | flops | bytes accessed | tf_op | source)
XLA Modules:
  0.0 20.5 jit_solution(16944981959620101031)
XLA Ops:
  0.7 19.2 %shard_map.82 = f32[3,8,8,128]{3,2,1,0:T(8,128)S(1)} custom-call(s32[1]{0:T(128)S(6)} %copy.10.lens, bf16[3,8,8,128]{3,2,1,0:T(8,128)(2,1)} %bitcast.13, bf16[1024,128]{1,0:T(8,128)(2,1)} %bitcast.11, bf16[1024,128]{1,0:T(8,128)(2,1)} %bitcast.12, bf16[1024,4,2,128]{3,2,1,0:T(2,128)(2,1)} %bitcast.9, bf16[1024,4,2,128]{3,2,1,0:T(2,128)(2,1)} %bitcast.10, ...), custom_call_target="tpu_custom_call" | custom-call | tf_op jit(solution)/shard_map/pallas_call | solution.py:361
  19.9 0.6 %copy.11 = f32[1,3,64,128]{3,2,1,0:T(8,128)} copy(f32[1,3,64,128]{3,2,1,0:T(8,128)S(1)} %bitcast.8) | data formatting | bytes 196608

commit v5 on v2

--- a/solution.py
+++ b/solution.py
@@ -22,10 +22,10 @@
 
 
 def kernel(
-    n, group, chunk,
+    n, group,
     lens, q_hbm, pk_hbm, pv_hbm, sk_hbm, sv_hbm, nk_hbm, nv_hbm,
     out_ref,
-    q_own, pk, pv, wide, k_send, v_send, q_all, k_all, v_all, sk, sv, nk, nv, s_own,
+    q_own, pk, pv, wide, k_send, v_send, q_all, k_all, v_all, sk, sv, nk, nv, s_own, hide,
     o_send, l_send, o_all, l_all, w_high, w_low, log_all, total_all,
     local_sem, suf_sem, late_sem, block_sem, q_ss, q_rs, k_ss, k_rs, v_ss, v_rs, o_ss, o_rs, l_ss, l_rs,
 ):
@@ -37,7 +37,7 @@
     head = lax.rem(me, kvh)
     mine = lax.div(me, kvh)
     base = me - head
-    chunks = sk.shape[0] // chunk
+    couples, suffix = sk.shape[:2]
     blocks = n // kvh
 
     def remote(src, dst, ss, rs, dev):
@@ -95,13 +95,10 @@
         c.start()
     own_q = pltpu.make_async_copy(q_hbm.at[:, head], q_all.at[me], q_rs.at[mine])
     own_q.start()
-    halves = []
-    for i, (a, b) in enumerate([(sk_hbm, sk), (sv_hbm, sv)]):
-        for c in range(chunks):
-            part = pl.ds(c * chunk, chunk)
-            halves.append(
-                pltpu.make_async_copy(a.at[part], b.at[part], suf_sem.at[i * chunks + c])
-            )
+    halves = [
+        pltpu.make_async_copy(a.at[:, c], b.at[c], suf_sem.at[i * couples + c])
+        for i, (a, b) in enumerate([(sk_hbm, sk), (sv_hbm, sv)]) for c in range(couples)
+    ]
     for c in halves:
         c.start()
 
@@ -173,17 +170,19 @@
     lane_head = lax.rem(lane, kvh)
     match = (row >= lane_head * per) & (row < (lane_head + 1) * per)
     bias = jnp.where(match, 0.0, -jnp.inf).astype(F32)
-    bias_wide = jnp.concatenate([bias] * (chunk // 128), axis=1)
-    token_of = lax.div(lax.broadcasted_iota(jnp.int32, (8, chunk), 1), kvh)
-
-    top = jnp.full((rows, 1), -jnp.inf, F32)
-    for c in range(chunks):
+    two = rows // couples
+    key = lax.broadcasted_iota(jnp.int32, (two, 2 * suffix), 1)
+    wide_row = lax.broadcasted_iota(jnp.int32, (two, 2 * suffix), 0)
+    seen = (lax.rem(key, 2) == lax.div(wide_row, per)) & (lax.div(key, 2) < length)
+    hide[...] = jnp.where(seen, 0.0, -jnp.inf).astype(F32)
+
+    tops = []
+    for c in range(couples):
         halves[c].wait()
-        s = nt_dot(q_rows, sk[c * chunk:(c + 1) * chunk, :]) * factor
-        limit = jnp.where(token_of < length - c * (chunk // kvh), 0.0, -jnp.inf).astype(F32)[:1]
-        s = s + bias_wide + limit
+        s = nt_dot(q_rows[c * two:(c + 1) * two], sk[c].reshape(2 * suffix, dim)) * factor + hide[...]
         s_own[c] = s
-        top = jnp.maximum(top, jnp.max(s, axis=-1, keepdims=True))
+        tops.append(jnp.max(s, axis=-1, keepdims=True))
+    top = jnp.concatenate(tops, axis=0)
 
     pad = jnp.zeros((128 - steps * kvh, dim), F32)
     new_k = jnp.concatenate([nk[j].astype(F32) for j in range(steps)] + [pad], axis=0).astype(BF16)
@@ -195,13 +194,16 @@
     w_new = jnp.exp(s_new - own_max)
     own_total = jnp.sum(w_new, axis=-1, keepdims=True)
     own_sum = jnp.dot(w_new.astype(BF16), new_v, preferred_element_type=F32)
-    for c in range(chunks):
-        halves[chunks + c].wait()
-        w = jnp.exp(s_own[c] - own_max)
-        own_total = own_total + jnp.sum(w, axis=-1, keepdims=True)
-        own_sum = own_sum + jnp.dot(
-            w.astype(BF16), sv[c * chunk:(c + 1) * chunk, :], preferred_element_type=F32
-        )
+    totals, sums_of = [], []
+    for c in range(couples):
+        halves[couples + c].wait()
+        w = jnp.exp(s_own[c] - own_max[c * two:(c + 1) * two])
+        totals.append(jnp.sum(w, axis=-1, keepdims=True))
+        sums_of.append(jnp.dot(
+            w.astype(BF16), sv[c].reshape(2 * suffix, dim), preferred_element_type=F32
+        ))
+    own_total = own_total + jnp.concatenate(totals, axis=0)
+    own_sum = own_sum + jnp.concatenate(sums_of, axis=0)
 
     def settle(ref, sem):
         pltpu.make_async_copy(ref, ref, sem).wait()
@@ -280,7 +282,7 @@
 
         repeat(0, groups, body)
 
-    repeat(1, blocks + 1, lambda b: emit(lax.rem(mine + b, blocks)))
+    repeat(1, blocks + 1, lambda b: emit(b - 1))
 
     highest, upper, lower = own_max, own_sum, own_total
     for r in range(blocks):
@@ -325,11 +327,9 @@
         suffix = sk.shape[1]
         per = steps * gsize
         group = math.gcd(kvh, 4)
-        chunk = math.gcd(suffix * kvh, 1024)
-        chunks = suffix * kvh // chunk
         dma = pltpu.SemaphoreType.DMA
         out = pl.pallas_call(
-            functools.partial(kernel, n, group, chunk),
+            functools.partial(kernel, n, group),
             out_shape=jax.ShapeDtypeStruct((steps, kvh, gsize, dim), F32),
             in_specs=[pl.BlockSpec(memory_space=pltpu.SMEM)]
             + [pl.BlockSpec(memory_space=pltpu.HBM)] * 7,
@@ -344,11 +344,12 @@
                 pltpu.VMEM((n, steps, gsize, dim), BF16),
                 pltpu.VMEM((kvh, tokens, dim), BF16),
                 pltpu.VMEM((kvh, tokens, dim), BF16),
-                pltpu.VMEM((suffix * kvh, dim), BF16),
-                pltpu.VMEM((suffix * kvh, dim), BF16),
+                pltpu.VMEM((kvh // 2, suffix, 2, dim), BF16),
+                pltpu.VMEM((kvh // 2, suffix, 2, dim), BF16),
                 pltpu.VMEM((steps, kvh, dim), BF16),
                 pltpu.VMEM((steps, kvh, dim), BF16),
-                pltpu.VMEM((chunks, kvh * per, chunk), F32),
+                pltpu.VMEM((kvh // 2, 2 * per, 2 * suffix), F32),
+                pltpu.VMEM((2 * per, 2 * suffix), F32),
                 pltpu.VMEM((n, steps, gsize, dim), I16),
                 pltpu.VMEM((n, 1, 128), F32),
                 pltpu.VMEM((n, steps, gsize, dim), I16),
@@ -357,7 +358,7 @@
                 pltpu.VMEM((n * per, kvh * tokens), BF16),
                 pltpu.VMEM((n * per, 1), F32),
                 pltpu.VMEM((n * per, 1), F32),
-                dma((5,)), dma((2 * chunks,)),
+                dma((5,)), dma((kvh,)),
                 pltpu.SemaphoreType.REGULAR, pltpu.SemaphoreType.REGULAR,
                 dma, dma((n // kvh,)), dma, dma, dma, dma,
                 dma, dma((n // kvh,)), dma, dma((n // kvh,)),
@@ -369,8 +370,8 @@
             queries.reshape(steps, kvh, gsize, dim),
             pk.reshape(tokens * kvh, dim),
             pv.reshape(tokens * kvh, dim),
-            sk.reshape(suffix * kvh, dim),
-            sv.reshape(suffix * kvh, dim),
+            sk.reshape(suffix, kvh // 2, 2, dim),
+            sv.reshape(suffix, kvh // 2, 2, dim),
             nk.reshape(steps, kvh, dim),
             nv.reshape(steps, kvh, dim),
         )])

time: 20.7 us -> 20.7 us (level)
  no operation moved by 1% of the time
where the time goes in v5:
time: 20.7 us; the launch traced here: 20.6 us
  Pallas kernels  19.3 us (93%)
  between operations  0.66 us (3%)
  local copies, waits for them, and re-layouts  0.64 us (3%)
    pallas_call x1, Pallas kernels, shards(): pl.pallas_call(functools.partial(kernel, n, group), out_shape=jax.ShapeDt...  19.3 us
    unnamed x1, local copies, waits for them, and re-layouts  0.64 us

profile of v5, /device:TPU:0, one launch (start us, length us, event | category | flops | bytes accessed | tf_op | source)
XLA Modules:
  0.0 20.6 jit_solution(13227121628722044658)
XLA Ops:
  0.7 19.3 %shard_map.82 = f32[3,8,8,128]{3,2,1,0:T(8,128)S(1)} custom-call(s32[1]{0:T(128)S(6)} %copy.10.lens, bf16[3,8,8,128]{3,2,1,0:T(8,128)(2,1)} %bitcast.13, bf16[1024,128]{1,0:T(8,128)(2,1)} %bitcast.11, bf16[1024,128]{1,0:T(8,128)(2,1)} %bitcast.12, bf16[1024,4,2,128]{3,2,1,0:T(2,128)(2,1)} %bitcast.9, bf16[1024,4,2,128]{3,2,1,0:T(2,128)(2,1)} %bitcast.10, ...), custom_call_target="tpu_custom_call" | custom-call | tf_op jit(solution)/shard_map/pallas_call | solution.py:331
  19.9 0.6 %copy.11 = f32[1,3,64,128]{3,2,1,0:T(8,128)} copy(f32[1,3,64,128]{3,2,1,0:T(8,128)S(1)} %bitcast.8) | data formatting | bytes 196608

commit v6 on v5

--- a/solution.py
+++ b/solution.py
@@ -223,20 +223,20 @@
     def weigh(block):
         settle(q_all.at[pl.ds(block * kvh, kvh)], q_rs.at[block])
 
-        def body(i):
-            first, at = place(block, i)
-            q_block = rows_of(q_all[pl.ds(first, group)]).astype(BF16)
-            s = nt_dot(q_block, keys) * factor
+        if True:
+            first = block * kvh
+            at = pl.ds(pl.multiple_of(first * per, kvh * per), kvh * per)
+            q_block = rows_of(q_all[pl.ds(first, kvh)]).astype(BF16)
+            s = nt_dot(q_block, keys)
             m = jnp.max(s, axis=-1, keepdims=True)
-            w = jnp.exp(s - m)
+            w = jnp.exp2((s - m) * (factor * math.log2(math.e)))
             total = jnp.sum(w, axis=-1, keepdims=True)
             high = w.astype(BF16)
             w_high[at] = high
             w_low[at] = (w - high.astype(F32)).astype(BF16)
             total_all[at] = total
-            log_all[at] = m + jnp.log(total)
-
-        repeat(0, groups, body)
+            log_all[at] = m * factor + jnp.log(total)
+
 
     repeat(0, blocks, lambda b: weigh(lax.rem(mine + b, blocks)))
 

time: 20.7 us -> 20.7 us (level)
  no operation moved by 1% of the time
where the time goes in v6:
time: 20.7 us; the launch traced here: 20.6 us
  Pallas kernels  19.3 us (93%)
  between operations  0.66 us (3%)
  local copies, waits for them, and re-layouts  0.64 us (3%)
    pallas_call x1, Pallas kernels, shards(): pl.pallas_call(functools.partial(kernel, n, group), out_shape=jax.ShapeDt...  19.3 us
    unnamed x1, local copies, waits for them, and re-layouts  0.64 us

profile of v6, /device:TPU:0, one launch (start us, length us, event | category | flops | bytes accessed | tf_op | source)
XLA Modules:
  0.0 20.6 jit_solution(8313508804947650516)
XLA Ops:
  0.7 19.3 %shard_map.82 = f32[3,8,8,128]{3,2,1,0:T(8,128)S(1)} custom-call(s32[1]{0:T(128)S(6)} %copy.10.lens, bf16[3,8,8,128]{3,2,1,0:T(8,128)(2,1)} %bitcast.13, bf16[1024,128]{1,0:T(8,128)(2,1)} %bitcast.11, bf16[1024,128]{1,0:T(8,128)(2,1)} %bitcast.12, bf16[1024,4,2,128]{3,2,1,0:T(2,128)(2,1)} %bitcast.9, bf16[1024,4,2,128]{3,2,1,0:T(2,128)(2,1)} %bitcast.10, ...), custom_call_target="tpu_custom_call" | custom-call | tf_op jit(solution)/shard_map/pallas_call | solution.py:331
  19.9 0.6 %copy.11 = f32[1,3,64,128]{3,2,1,0:T(8,128)} copy(f32[1,3,64,128]{3,2,1,0:T(8,128)S(1)} %bitcast.8) | data formatting | bytes 196608
